TPU v7x, 32 devices: a whole 2x2x4 slice. The times are simulated.
32 devices in a mesh: dp: 8 (over z, x), expert: 4 (over y, core).
Axes of the slice: x: 2, y: 2, z: 4, core: 2. Of those that a mesh axis runs over, the one named last changes fastest.
Arguments:
- x_spans: bfloat16 [8, 8, 4, 16, 1536], P('dp', None, 'expert'), may hold values from -36 to 36
- crops: int32 [8, 4, 128, 1], P('dp', 'expert'), may hold values from 0 to 7; in each aligned block of 128 rows (0 to 127, 128 to 255, ..., all dimensions but the last counted through in order) at most 32 rows name the same one
- decay: float32 [8, 4, 128, 24], P('dp', 'expert'), may hold values from -1 to 0
- attn_gain: bfloat16 [1536], replicated, may hold values from 0.099609375 to 1.8984375
- w_query: bfloat16 [1536, 1536], replicated, may hold values from -0.15625 to 0.15625
- w_key: bfloat16 [1536, 1536], replicated, may hold values from -0.15625 to 0.15625
- w_value: bfloat16 [1536, 1536], replicated, may hold values from -0.15625 to 0.15625
- head_gain: bfloat16 [1536], replicated, may hold values from 0.099609375 to 1.8984375
- w_out: bfloat16 [1536, 1536], replicated, may hold values from -0.15625 to 0.15625
- moe_gain: bfloat16 [1536], replicated, may hold values from 0.099609375 to 1.8984375
- w_gate: bfloat16 [8, 1536, 6144], P('expert', None, 'dp'), may hold values from -0.15625 to 0.15625
- w_up: bfloat16 [8, 1536, 6144], P('expert', None, 'dp'), may hold values from -0.15625 to 0.15625
- w_down: bfloat16 [8, 6144, 1536], P('expert', 'dp'), may hold values from -0.078125 to 0.078125
Outputs:
- layer_out: bfloat16 [8, 4, 128, 1536], P('dp', 'expert')
Inputs may be any that keep to these rules, and one draw needn't show every extreme that they name: `crops`: within the tokens of one plot no crop is named more than 32 times, and some plot names some crop exactly 32 times.
All inputs are finite; a program needn't handle non-finite values.
Results may differ from a plain program's by a relative error of at most 0.012.
Values may be sent and summed in bfloat16 or wider, within the bound.
A program may use at most 128 MiB of HBM per device.

v0:
```python
import jax
import jax.numpy as jnp
from jax import lax
from jax.sharding import PartitionSpec as P

D = 1536
HEADS = 24
HEAD_DIM = 64
EXPERTS = 8
SPAN = 64


def rms_scale(values, width_eps):
    return lax.rsqrt(jnp.mean(values * values, axis=-1, keepdims=True) + width_eps)


def spread(buffers):
    return lax.all_gather(buffers, "dp", axis=0, tiled=True)


def deliver(buffers):
    return lax.all_to_all(buffers, "expert", split_axis=1, concat_axis=1, tiled=True)


def linear_mixing(query, key_vecs, value_vecs, forget, length):
    blocks = length // SPAN
    query_narrow = query.reshape(blocks, SPAN, HEADS, HEAD_DIM)
    key_narrow = key_vecs.reshape(blocks, SPAN, HEADS, HEAD_DIM)
    query_blocks = query_narrow.astype(jnp.float32)
    key_blocks = key_narrow.astype(jnp.float32)
    value_blocks = value_vecs.astype(jnp.float32).reshape(blocks, SPAN, HEADS, HEAD_DIM)
    within = jnp.cumsum(forget.reshape(blocks, SPAN, HEADS), axis=1)
    block_total = within[:, -1, :]
    scores = jnp.einsum(
        "nthd,nshd->nhts", query_narrow, key_narrow, preferred_element_type=jnp.float32
    )
    by_head = jnp.transpose(within, (0, 2, 1))
    spread_vals = by_head[:, :, :, None] - by_head[:, :, None, :]
    causal = jnp.arange(SPAN)[:, None] >= jnp.arange(SPAN)[None, :]
    weights = jnp.exp(jnp.where(causal[None, None], spread_vals, -jnp.inf))
    local_part = jnp.einsum(
        "nhts,nshd->nthd", scores * weights, value_blocks, precision=lax.Precision.HIGHEST
    )
    carried_keys = key_blocks * jnp.exp(block_total[:, None, :] - within)[..., None]
    block_states = jnp.einsum(
        "nshd,nshe->nhde", carried_keys, value_blocks, precision=lax.Precision.HIGHEST
    )

    def advance(carried, element):
        block_state, total_now = element
        return (carried * jnp.exp(total_now)[:, None, None] + block_state, carried)

    _, entering = lax.scan(
        advance, jnp.zeros((HEADS, HEAD_DIM, HEAD_DIM), jnp.float32), (block_states, block_total)
    )
    earlier_part = jnp.einsum(
        "nthd,nhde->nthe",
        query_blocks * jnp.exp(within)[..., None],
        entering,
        precision=lax.Precision.HIGHEST,
    )
    return (local_part + earlier_part).reshape(length, HEADS, HEAD_DIM)


def on_device(
    x_spans,
    crops,
    decay,
    attn_gain,
    w_query,
    w_key,
    w_value,
    head_gain,
    w_out,
    moe_gain,
    w_gate,
    w_up,
    w_down,
):
    arrived = lax.all_to_all(x_spans, "dp", split_axis=1, concat_axis=0, tiled=True)
    length = arrived.shape[0] * arrived.shape[3]
    tokens = arrived.reshape(length, D)
    forget = decay.reshape(length, HEADS)
    widened = tokens.astype(jnp.float32)
    normed = (widened * rms_scale(widened, 1e-05) * attn_gain.astype(jnp.float32)).astype(
        jnp.bfloat16
    )
    query = jnp.dot(normed, w_query, preferred_element_type=jnp.float32).astype(jnp.bfloat16)
    key_vecs = jnp.dot(normed, w_key, preferred_element_type=jnp.float32).astype(jnp.bfloat16)
    value_vecs = jnp.dot(normed, w_value, preferred_element_type=jnp.float32).astype(jnp.bfloat16)
    mixed = linear_mixing(query, key_vecs, value_vecs, forget, length)
    head_scale = head_gain.astype(jnp.float32).reshape(HEADS, HEAD_DIM)
    head_normed = (
        (mixed * rms_scale(mixed, 1e-05) * head_scale).reshape(length, D).astype(jnp.bfloat16)
    )
    resid = (widened + jnp.dot(head_normed, w_out, preferred_element_type=jnp.float32)).astype(
        jnp.bfloat16
    )
    resid_wide = resid.astype(jnp.float32)
    routed = (resid_wide * rms_scale(resid_wide, 1e-05) * moe_gain.astype(jnp.float32)).astype(
        jnp.bfloat16
    )
    crop_ids = crops.reshape(length)
    onehot = (crop_ids[:, None] == jnp.arange(EXPERTS, dtype=jnp.int32)[None, :]).astype(jnp.int32)
    slot_ids = jnp.sum((jnp.cumsum(onehot, axis=0) - onehot) * onehot, axis=1)
    capacity = length // 4
    position = crop_ids * capacity + slot_ids
    select = (jnp.arange(EXPERTS * capacity, dtype=jnp.int32)[:, None] == position[None, :]).astype(
        jnp.bfloat16
    )
    packed = jnp.dot(select, routed, preferred_element_type=jnp.float32).astype(jnp.bfloat16)
    owners = lax.axis_size("expert")
    local_count = w_gate.shape[0]
    outgoing = packed.reshape(1, owners, EXPERTS * capacity // owners, D)
    gathered = spread(deliver(outgoing))
    sources = gathered.shape[0]
    grouped = gathered.reshape(sources, owners, local_count, capacity, D)
    gate_act = jnp.einsum("sojcd,jdf->sojcf", grouped, w_gate, preferred_element_type=jnp.float32)
    up_act = jnp.einsum("sojcd,jdf->sojcf", grouped, w_up, preferred_element_type=jnp.float32)
    hidden = (jax.nn.silu(gate_act) * up_act).astype(jnp.bfloat16)
    term = jnp.einsum("sojcf,jfd->sojcd", hidden, w_down, preferred_element_type=jnp.float32)
    summed = lax.psum_scatter(
        term.reshape(1 * lax.axis_size("dp"), owners, local_count * capacity, D).astype(
            jnp.bfloat16
        ),
        "dp",
        scatter_dimension=0,
        tiled=True,
    )
    own_sums = summed[0]
    returned = lax.all_to_all(own_sums, "expert", split_axis=0, concat_axis=0, tiled=True)
    flat_back = returned.reshape(EXPERTS * capacity, D)
    expert_out = jnp.einsum("pl,pd->ld", select, flat_back, preferred_element_type=jnp.float32)
    layer_sum = (resid_wide + expert_out).astype(jnp.bfloat16)
    return layer_sum.reshape(1, 1, length, D)


def solution(mesh):
    return jax.shard_map(
        on_device,
        mesh=mesh,
        in_specs=(
            P("dp", None, "expert", None, None),
            P("dp", "expert", None, None),
            P("dp", "expert", None, None),
            P(),
            P(),
            P(),
            P(),
            P(),
            P(),
            P(),
            P("expert", None, "dp"),
            P("expert", None, "dp"),
            P("expert", "dp", None),
        ),
        out_specs=P("dp", "expert", None, None),
        check_vma=False,
    )
```

profile of v0, /device:TPU:0, one launch (start us, length us, event | category | flops | bytes accessed | tf_op | source)
XLA Modules:
  0.0 337.4 jit_solution(17913030399810466076)
XLA Ops:
  6.5 7.3 %all-to-all-start = ((bf16[1,8,1,16,1536]{4,3,2,0,1:T(8,128)(2,1)}), bf16[1,8,1,16,1536]{4,3,2,0,1:T(8,128)(2,1)S(1)}, u32[]{:S(2)}, u32[]{:S(2)}) async-start(bf16[1,8,1,16,1536]{4,3,2,0,1:T(8,128)(2,1)} %bitcast.97), calls=%async_computation | async-start | bytes 786432 | tf_op jit(solution)/shard_map/all_to_all | solution.py:80
  21.2 1.2 multiply_add_fusion
  22.5 3.0 all-to-all-done
  25.9 3.1 convolution_convert_fusion.1
  30.0 3.1 convolution_convert_fusion.2
  33.2 3.1 convolution_convert_fusion.3
  36.3 1.3 reshape.128
  39.0 1.5 fusion.45
  40.5 2.2 fusion.24
  42.6 3.8 %while.13 = (s32[]{:T(128)}, f32[24,64,64]{2,1,0:T(8,128)S(1)}, f32[2,24,64,64]{3,2,1,0:T(8,128)}, f32[2,24]{1,0:T(2,128)}, f32[2,24,64,64]{3,2,1,0:T(8,128)S(1)}, /*index=5*/s32[]{:T(128)}, s32[]{:T(128)}) while((s32[]{:T(128)}, f32[24,64,64]{2,1,0:T(8,128)S(1)}, f32[2,24,64,64]{3,2,1,0:T(8,128)}, f32[2,24]{1,0:T(2,128)}, ...), condition=%wide.region_3.4_spmd.clone, body=%wide.region_2.3_spmd.clone.sunk | while | flops 393219 | bytes 2359692 | solution.py:53
  43.6 1.0 bitcast_dynamic-update-slice_fusion.2
  46.5 3.6 %fusion.27 = f32[2,24,64,64]{3,2,1,0:T(8,128)S(1)} fusion(f32[2,24,64,64]{3,2,1,0:T(8,128)} %fusion.45, f32[2,24,64]{2,1,0:T(8,128)} %copy.56, pred[64,64]{1,0:T(8,128)(4,1)} %iota_compare_fusion.4, bf16[2,64,24,64]{3,2,1,0:T(8,128)(2,1)} %reshape.128), kind=kOutput, calls=%fused_computation.38 | convolution fusion | flops 151584768 | bytes 1982464 | tf_op jit(solution)/shard_map/nhts,nshd->nthd/dot_general | solution.py:41
  50.1 3.9 %multiply_reduce_fusion = (f32[2,64,24]{1,2,0:T(8,128)S(1)}, f32[2,64,24,64]{1,3,2,0:T(8,128)S(1)}) fusion(f32[2,24,64,64]{3,2,1,0:T(8,128)S(1)} %fusion.27, f32[2,24,64,64]{3,2,1,0:T(8,128)S(1)} %copy-done.2, f32[2,64,24]{1,2,0:T(8,128)} %copy.63, bf16[2,64,24,64]{3,2,1,0:T(8,128)(2,1)S(1)} %copy-done.1), kind=kOutput, calls=%fused_computation.30 | convolution fusion | flops 151974912 | bytes 2777088 | tf_op jit(solution)/shard_map/nthd,nhde->nthe/dot_general | solution.py:56
  54.2 1.1 copy.67
  56.3 3.5 %multiply_reduce_fusion.1 = (f32[128]{0:T(128)S(1)}, f32[128,1536]{1,0:T(8,128)S(1)}) fusion(bf16[1536,1536]{1,0:T(8,128)(2,1)} %param.23, f32[128,1536]{1,0:T(8,128)S(1)} %reshape.131, f32[128,1536]{1,0:T(8,128)} %copy.67, f32[1536]{0:T(1024)S(1)} %convert_element_type.84, bf16[128,1536]{1,0:T(8,128)(2,1)S(1)} %bitcast.90), kind=kOutput, calls=%fused_computation.47 | convolution fusion | flops 605749120 | bytes 7477760 | tf_op jit(solution)/shard_map/dot_general | solution.py:96
  60.2 14.8 %all_to_all.19 = bf16[1,4,64,1536]{3,2,0,1:T(8,128)(2,1)} all-to-all(bf16[1,4,64,1536]{3,2,0,1:T(8,128)(2,1)S(1)} %bitcast.94), channel_id=1, replica_groups=mesh['dp'=8,'expert'=4] {'expert'}, dimensions={1} | all-to-all | bytes 1572864 | tf_op jit(solution)/shard_map/all_to_all | solution.py:22
  75.1 97.2 %all-gather.2.cloned.1.call-done = bf16[8,4,64,1536]{3,2,1,0:T(8,128)(2,1)} async-done(((bf16[1,4,64,1536]{3,2,1,0:T(8,128)(2,1)}), bf16[8,4,64,1536]{3,2,1,0:T(8,128)(2,1)}) %all-gather.2.cloned.1.call-update) | async-done | bytes 6291472 | tf_op jit(solution)/shard_map/all_gather | solution.py:18
  172.3 8.7 %fusion.6 = f32[2,8,4,32,768]{4,3,2,1,0:T(8,128)S(1)} fusion(bf16[8,4,2,32,1536]{4,3,2,1,0:T(8,128)(2,1)} %bitcast.103, bf16[2,1536,768]{2,1,0:T(8,128)(2,1)} %param.26), kind=kOutput, calls=%fused_computation.13 | convolution fusion | flops 4831838208 | bytes 17301504 | tf_op jit(solution)/shard_map/sojcd,jdf->sojcf/dot_general | solution.py:119
  181.0 8.4 %fusion.2 = bf16[8,4,2,32,768]{4,3,1,0,2:T(8,128)(2,1)S(1)} fusion(f32[2,8,4,32,768]{4,3,2,1,0:T(8,128)S(1)} %fusion.6, bf16[2,1536,768]{2,1,0:T(8,128)(2,1)} %param.25, bf16[8,4,2,32,1536]{4,3,2,1,0:T(8,128)(2,1)S(1)} %bitcast.104), kind=kOutput, calls=%fused_computation.6 | convolution fusion | flops 4841275392 | bytes 20447232 | tf_op jit(solution)/shard_map/sojcd,jdf->sojcf/dot_general | solution.py:118
  189.4 5.2 %convert_bitcast_fusion = bf16[8,4,2,32,1536]{4,3,1,0,2:T(8,128)(2,1)S(1)} fusion(bf16[8,4,2,32,768]{4,3,1,0,2:T(8,128)(2,1)S(1)} %fusion.2, bf16[2,768,1536]{2,1,0:T(8,128)(2,1)S(1)} %bitcast.106), kind=kOutput, calls=%fused_computation.12 | convolution fusion | flops 4834983936 | bytes 14155776 | tf_op jit(solution)/shard_map/sojcf,jfd->sojcd/dot_general | solution.py:121
  194.7 3.4 %copy.72 = bf16[8,4,2,32,1536]{4,3,2,1,0:T(8,128)(2,1)} copy(bf16[8,4,2,32,1536]{4,3,1,0,2:T(8,128)(2,1)S(1)} %convert_bitcast_fusion) | data formatting | bytes 12582912 | tf_op jit(solution)/shard_map/convert_element_type | solution.py:123
  198.1 116.3 %reduce-scatter.2.cloned.1.call-done = bf16[1,4,64,1536]{3,2,1,0:T(8,128)(2,1)} async-done(((bf16[8,4,64,1536]{3,2,1,0:T(8,128)(2,1)}), bf16[1,4,64,1536]{3,2,1,0:T(8,128)(2,1)}) %reduce-scatter.2.cloned.1.call-update) | async-done | bytes 786448 | tf_op jit(solution)/shard_map/reduce_scatter | solution.py:122
  314.4 15.1 %all_to_all.20 = bf16[4,64,1536]{2,1,0:T(8,128)(2,1)S(1)} all-to-all(bf16[4,64,1536]{2,1,0:T(8,128)(2,1)} %bitcast.95), channel_id=1, replica_groups=mesh['dp'=8,'expert'=4] {'expert'}, dimensions={0} | all-to-all | bytes 1572864 | tf_op jit(solution)/shard_map/all_to_all | solution.py:131
  329.5 1.1 fusion.20
  (57 shorter events, 14.4 us)
Async XLA Ops:
  6.5 18.9 %all-to-all-start = ((bf16[1,8,1,16,1536]{4,3,2,0,1:T(8,128)(2,1)}), bf16[1,8,1,16,1536]{4,3,2,0,1:T(8,128)(2,1)S(1)}, u32[]{:S(2)}, u32[]{:S(2)}) async-start(bf16[1,8,1,16,1536]{4,3,2,0,1:T(8,128)(2,1)} %bitcast.97), calls=%async_computation | async-start | bytes 786432 | tf_op jit(solution)/shard_map/all_to_all | solution.py:80
  13.8 158.5 %all-gather.2.cloned.1.call-start = ((), (), s32[]{:S(2)}) async-start(), calls=%async_computation.4 | async-start | bytes 7077888 | tf_op jit(solution)/shard_map/all_gather | solution.py:18
  17.6 8.1 %copy-start.3 = (f32[2,1,24]{2,1,0:T(1,128)}, f32[2,1,24]{2,1,0:T(1,128)S(1)}, u32[]{:S(2)}) copy-start(f32[2,1,24]{2,1,0:T(1,128)S(1)} %slice.4) | copy-start | bytes 580
  38.1 0.9 copy-start
  42.6 7.4 %copy-start.1 = (bf16[2,64,24,64]{3,2,1,0:T(8,128)(2,1)S(1)}, bf16[2,64,24,64]{3,2,1,0:T(8,128)(2,1)}, u32[]{:S(2)}) copy-start(bf16[2,64,24,64]{3,2,1,0:T(8,128)(2,1)} %copy-done) | copy-start | bytes 1179652
  46.5 3.6 %copy-start.2 = (f32[2,24,64,64]{3,2,1,0:T(8,128)S(1)}, f32[2,24,64,64]{3,2,1,0:T(8,128)}, u32[]{:S(2)}) copy-start(f32[2,24,64,64]{3,2,1,0:T(8,128)} %get-tuple-element.32) | copy-start | bytes 2359300
  55.9 3.9 %copy-start.4 = (s32[128]{0:T(128)S(1)}, s32[128]{0:T(128)}, u32[]{:S(2)}) copy-start(s32[128]{0:T(128)} %multiply_add_fusion) | copy-start | bytes 1540
  75.0 239.4 %reduce-scatter.2.cloned.1.call-start = ((), (), s32[]{:S(2)}) async-start(), calls=%async_computation.5 | async-start | bytes 7077888 | tf_op jit(solution)/shard_map/reduce_scatter | solution.py:122
  172.3 8.7 %copy-start.5 = (bf16[8,4,64,1536]{3,2,1,0:T(8,128)(2,1)S(1)}, bf16[8,4,64,1536]{3,2,1,0:T(8,128)(2,1)}, u32[]{:S(2)}) copy-start(bf16[8,4,64,1536]{3,2,1,0:T(8,128)(2,1)} %all-gather.2.cloned.1.call-done) | copy-start | bytes 18874372
  172.3 17.1 %slice-start = ((s8[4718592]{0:T(1024)(128)(4,1)}), s8[4194304]{0:T(1024)(128)(4,1)S(1)}, s32[]{:S(2)}) async-start(s8[4718592]{0:T(1024)(128)(4,1)} %bitcast.105), calls=%async_computation.6 | async-start | bytes 8388608
  181.0 8.4 %slice-start.1 = ((s8[4718592]{0:T(1024)(128)(4,1)}), s8[524288]{0:T(1024)(128)(4,1)S(1)}, s32[]{:S(2)}) async-start(s8[4718592]{0:T(1024)(128)(4,1)} %bitcast.105), calls=%async_computation.7 | async-start | bytes 1048576
Sparse Core Ops, SparseCore 0:
  75.2 97.1 all-gather.1
  198.2 116.1 reduce-scatter.1
where the time goes:
time: 338 us; the launch traced here: 337 us
  waiting for transfers between devices  217 us (64%)
  matrix products  47.8 us (14%)
  blocking collectives  29.9 us (9%)
  between operations  13.7 us (4%)
  local copies, waits for them, and re-layouts  13.6 us (4%)
  other arithmetic  8.3 us (2%)
  starting transfers between devices  7.33 us (2%)
    reduce_scatter x1, waiting for transfers between devices, on_device(): lax.psum_scatter(term.reshape(1 * lax.axis_size('dp'), owners, local_coun...  116 us
    all_gather x1, waiting for transfers between devices, spread(): return lax.all_gather(buffers, 'dp', axis=0, tiled=True)  97.2 us
    all_to_all x1, blocking collectives, on_device(): lax.all_to_all(own_sums, 'expert', split_axis=0, concat_axis=0, tiled=True)  15.1 us
    all_to_all x1, blocking collectives, deliver(): lax.all_to_all(buffers, 'expert', split_axis=1, concat_axis=1, tiled=True)  14.8 us
    dot_general x1, matrix products, on_device(): jnp.einsum('sojcd,jdf->sojcf', grouped, w_up, preferred_element_type=jnp....  8.68 us
    dot_general x1, matrix products, on_device(): jnp.einsum('sojcd,jdf->sojcf', grouped, w_gate, preferred_element_type=jn...  8.37 us
    all_to_all x1, starting transfers between devices, on_device(): lax.all_to_all(x_spans, 'dp', split_axis=1, concat_axis=0, tiled=True)  7.25 us
  transfers between devices with their start and end apart: 3, of which 3 were waited for; matrix products, arithmetic and copies ran while one was open for 3% of the time, Pallas kernels for 0%

commit v1 on v0

--- a/solution.py
+++ b/solution.py
@@ -10,12 +10,38 @@
 SPAN = 64
 
 
+def _find_lots_all(q_in, axis_k):
+    q_in = jnp.moveaxis(q_in, 0, axis_k)
+    clean = q_in.shape
+    return q_in.reshape(*clean[:axis_k], clean[axis_k] * clean[axis_k + 1], *clean[axis_k + 2 :])
+
+
 def rms_scale(values, width_eps):
     return lax.rsqrt(jnp.mean(values * values, axis=-1, keepdims=True) + width_eps)
 
 
 def spread(buffers):
-    return lax.all_gather(buffers, "dp", axis=0, tiled=True)
+
+    def _play_shapes(sheet, dev_axis, out_dim):
+        chips = lax.axis_size(dev_axis)
+        vals = [(u, (u + 1) % chips) for u in range(chips)]
+        shelf = [(d, j0) for j0, d in vals]
+        right_arr, block_now = ([], [])
+        for k in tuple(range(chips - 1)):
+            if k % 2 == 0:
+                tall = lax.ppermute(right_arr[-1] if right_arr else sheet, dev_axis, vals)
+                right_arr.append(tall)
+            else:
+                now = lax.ppermute(block_now[-1] if block_now else sheet, dev_axis, shelf)
+                block_now.append(now)
+        tmp = jnp.stack([*right_arr[::-1], sheet, *block_now])
+        r_now = lax.axis_index(dev_axis)
+        v_next = len(right_arr)
+        shaped = r_now - v_next
+        tmp = tmp[(jnp.arange(chips) - shaped) % chips]
+        return _find_lots_all(tmp, out_dim)
+
+    return _play_shapes(buffers, "dp", 0)
 
 
 def deliver(buffers):

time: 338 us -> 380 us (1.12)
  starting transfers between devices: 7.33 us -> 51.2 us
  local copies, waits for them, and re-layouts: 13.6 us -> 30.9 us
  waiting for transfers between devices: 217 us -> 200 us
    all_gather x1 -> x0, waiting for transfers between devices: 97.2 us -> none  [spread(): return lax.all_gather(buffers, 'dp', axis=0, tiled=True)]
    ppermute x0 -> x7, waiting for transfers between devices: none -> 80.5 us  [the longest x4 80.5 us: _play_shapes(): tall = lax.ppermute(right_arr[-1] if right_arr else sheet, dev_axis, vals)]
    ppermute x0 -> x7, starting transfers between devices: none -> 43.9 us  [the longest x3 37.4 us: _play_shapes(): now = lax.ppermute(block_now[-1] if block_now else sheet, dev_axis, shelf)]
    unnamed x16 -> x33, local copies, waits for them, and re-layouts: 0.89 us -> 11.7 us
    gather x0 -> x1, local copies, waits for them, and re-layouts: none -> 6.39 us  [_play_shapes(): tmp = tmp[(jnp.arange(chips) - shaped) % chips]]
  transfers between devices with their start and end apart: 3 -> 9, of which waited for: 3 -> 6; matrix products, arithmetic and copies ran while one was open for 3% -> 5% of each run, Pallas kernels for 0% -> 0%
where the time goes in v1:
time: 380 us; the launch traced here: 379 us
  waiting for transfers between devices  200 us (53%)
  starting transfers between devices  51.2 us (13%)
  matrix products  44.9 us (12%)
  local copies, waits for them, and re-layouts  30.9 us (8%)
  blocking collectives  29.4 us (8%)
  between operations  13.8 us (4%)
  other arithmetic  8.98 us (2%)
    reduce_scatter x1, waiting for transfers between devices, on_device(): lax.psum_scatter(term.reshape(1 * lax.axis_size('dp'), owners, local_coun...  117 us
    ppermute x4, waiting for transfers between devices, _play_shapes(): tall = lax.ppermute(right_arr[-1] if right_arr else sheet, dev_axis, vals)  80.5 us
    ppermute x3, starting transfers between devices, _play_shapes(): now = lax.ppermute(block_now[-1] if block_now else sheet, dev_axis, shelf)  37.4 us
    all_to_all x1, blocking collectives, on_device(): lax.all_to_all(own_sums, 'expert', split_axis=0, concat_axis=0, tiled=True)  15.1 us
    all_to_all x1, blocking collectives, deliver(): lax.all_to_all(buffers, 'expert', split_axis=1, concat_axis=1, tiled=True)  14.2 us
    unnamed x33, local copies, waits for them, and re-layouts  11.7 us
    dot_general x1, matrix products, on_device(): jnp.einsum('sojcd,jdf->sojcf', grouped, w_up, preferred_element_type=jnp....  8.68 us
    dot_general x1, matrix products, on_device(): jnp.einsum('sojcd,jdf->sojcf', grouped, w_gate, preferred_element_type=jn...  8.37 us
  transfers between devices with their start and end apart: 9, of which 6 were waited for; matrix products, arithmetic and copies ran while one was open for 5% of the time, Pallas kernels for 0%

profile of v1, /device:TPU:0, one launch (start us, length us, event | category | flops | bytes accessed | tf_op | source)
XLA Modules:
  0.0 379.5 jit_solution(2762869376424258999)
XLA Ops:
  6.5 7.3 %all-to-all-start = ((bf16[1,8,1,16,1536]{4,3,2,0,1:T(8,128)(2,1)}), bf16[1,8,1,16,1536]{4,3,2,0,1:T(8,128)(2,1)S(1)}, u32[]{:S(2)}, u32[]{:S(2)}) async-start(bf16[1,8,1,16,1536]{4,3,2,0,1:T(8,128)(2,1)} %bitcast.118), calls=%async_computation | async-start | bytes 786432 | tf_op jit(solution)/shard_map/all_to_all | solution.py:106
  22.9 2.6 all-to-all-done
  25.9 3.3 convolution_convert_fusion.1
  30.2 3.1 convolution_convert_fusion.3
  36.8 3.8 %while.13 = (s32[]{:T(128)}, f32[24,64,64]{2,1,0:T(8,128)S(1)}, f32[2,24,64,64]{3,2,1,0:T(8,128)}, f32[2,24]{1,0:T(2,128)}, f32[2,24,64,64]{3,2,1,0:T(8,128)S(1)}, /*index=5*/s32[]{:T(128)}, s32[]{:T(128)}) while((s32[]{:T(128)}, f32[24,64,64]{2,1,0:T(8,128)S(1)}, f32[2,24,64,64]{3,2,1,0:T(8,128)}, f32[2,24]{1,0:T(2,128)}, ...), condition=%wide.region_3.4_spmd.clone, body=%wide.region_2.3_spmd.clone.sunk | while | flops 393219 | bytes 2360192 | solution.py:79
  40.7 3.3 convolution_convert_fusion.2
  46.7 3.8 multiply_reduce_fusion
  52.6 3.2 multiply_reduce_fusion.1
  56.3 14.2 %all_to_all.19 = bf16[1,4,64,1536]{3,2,0,1:T(8,128)(2,1)S(1)} all-to-all(bf16[1,4,64,1536]{3,2,0,1:T(8,128)(2,1)S(1)} %bitcast.115), channel_id=1, replica_groups=mesh['dp'=8,'expert'=4] {'expert'}, dimensions={1} | all-to-all | bytes 1572864 | tf_op jit(solution)/shard_map/all_to_all | solution.py:48
  72.1 20.1 %collective-permute-done = bf16[1,4,64,1536]{3,2,1,0:T(8,128)(2,1)S(1)} collective-permute-done((bf16[1,4,64,1536]{3,2,1,0:T(8,128)(2,1)S(1)}, bf16[1,4,64,1536]{3,2,1,0:T(8,128)(2,1)S(1)}, u32[]{:S(2)}, u32[]{:S(2)}) %collective-permute-start) | collective-permute-done | bytes 786464 | tf_op jit(solution)/shard_map/ppermute | solution.py:32
  92.2 4.7 %collective-permute-start.4 = (bf16[1,4,64,1536]{3,2,0,1:T(8,128)(2,1)S(1)}, bf16[1,4,64,1536]{3,2,0,1:T(8,128)(2,1)S(1)}, u32[]{:S(2)}, u32[]{:S(2)}) collective-permute-start(bf16[1,4,64,1536]{3,2,0,1:T(8,128)(2,1)S(1)} %all_to_all.19), channel_id=1, source_target_pairs={{4,0},{8,4},{12,8},{16,12},{20,16},{24,20},{28,24},{0,28},{5,1},{9... | collective-permute-start | bytes 2359304 | tf_op jit(solution)/shard_map/ppermute | solution.py:35
  96.9 27.9 %collective-permute-done.1 = bf16[1,4,64,1536]{3,2,1,0:T(8,128)(2,1)S(1)} collective-permute-done((bf16[1,4,64,1536]{3,2,1,0:T(8,128)(2,1)S(1)}, bf16[1,4,64,1536]{3,2,1,0:T(8,128)(2,1)S(1)}, u32[]{:S(2)}, u32[]{:S(2)}) %collective-permute-start.1) | collective-permute-done | bytes 786464 | tf_op jit(solution)/shard_map/ppermute | solution.py:32
  127.3 15.9 %collective-permute-start.5 = (bf16[1,4,64,1536]{3,2,0,1:T(8,128)(2,1)S(1)}, bf16[1,4,64,1536]{3,2,0,1:T(8,128)(2,1)}, u32[]{:S(2)}, u32[]{:S(2)}) collective-permute-start(bf16[1,4,64,1536]{3,2,0,1:T(8,128)(2,1)S(1)} %collective-permute-done.4), channel_id=1, source_target_pairs={{4,0},{8,4},{12,8},{16,12},{20,16},{24,20},{28,24},{0,28},{5,1},{9... | collective-permute-start | bytes 2359304 | tf_op jit(solution)/shard_map/ppermute | solution.py:35
  143.2 16.9 %collective-permute-done.2 = bf16[1,4,64,1536]{3,2,1,0:T(8,128)(2,1)} collective-permute-done((bf16[1,4,64,1536]{3,2,1,0:T(8,128)(2,1)S(1)}, bf16[1,4,64,1536]{3,2,1,0:T(8,128)(2,1)}, u32[]{:S(2)}, u32[]{:S(2)}) %collective-permute-start.2) | collective-permute-done | bytes 786464 | tf_op jit(solution)/shard_map/ppermute | solution.py:32
  160.2 2.6 collective-permute-start.3
  162.8 16.8 %collective-permute-start.6 = (bf16[1,4,64,1536]{3,2,0,1:T(8,128)(2,1)}, bf16[1,4,64,1536]{3,2,0,1:T(8,128)(2,1)S(1)}, u32[]{:S(2)}, u32[]{:S(2)}) collective-permute-start(bf16[1,4,64,1536]{3,2,0,1:T(8,128)(2,1)} %collective-permute-done.5), channel_id=1, source_target_pairs={{4,0},{8,4},{12,8},{16,12},{20,16},{24,20},{28,24},{0,28},{5,1},{9... | collective-permute-start | bytes 2359304 | tf_op jit(solution)/shard_map/ppermute | solution.py:35
  179.5 15.5 %collective-permute-done.3 = bf16[1,4,64,1536]{3,2,1,0:T(8,128)(2,1)} collective-permute-done((bf16[1,4,64,1536]{3,2,1,0:T(8,128)(2,1)}, bf16[1,4,64,1536]{3,2,1,0:T(8,128)(2,1)}, u32[]{:S(2)}, u32[]{:S(2)}) %collective-permute-start.3) | collective-permute-done | bytes 786464 | tf_op jit(solution)/shard_map/ppermute | solution.py:32
  207.1 6.4 %gather_fusion = bf16[8,4,64,1536]{3,2,1,0:T(8,128)(2,1)} fusion(bf16[8,4,64,1536]{3,2,1,0:T(8,128)(2,1)} %bitcast.19, s32[1024]{0:T(1024)S(1)} %pad_clamp_fusion), kind=kCustom, calls=%fused_computation | custom fusion | bytes 12582944 | tf_op jit(solution)/shard_map/gather | solution.py:41
  213.5 8.7 %fusion.6 = f32[2,8,4,32,768]{4,3,2,1,0:T(8,128)S(1)} fusion(bf16[8,4,2,32,1536]{4,3,2,1,0:T(8,128)(2,1)} %bitcast.110, bf16[2,1536,768]{2,1,0:T(8,128)(2,1)} %param.26), kind=kOutput, calls=%fused_computation.14 | convolution fusion | flops 4831838208 | bytes 17301504 | tf_op jit(solution)/shard_map/sojcd,jdf->sojcf/dot_general | solution.py:145
  222.2 8.4 %fusion.2 = bf16[8,4,2,32,768]{4,3,1,0,2:T(8,128)(2,1)S(1)} fusion(f32[2,8,4,32,768]{4,3,2,1,0:T(8,128)S(1)} %fusion.6, bf16[2,1536,768]{2,1,0:T(8,128)(2,1)} %param.25, bf16[8,4,2,32,1536]{4,3,2,1,0:T(8,128)(2,1)S(1)} %bitcast.111), kind=kOutput, calls=%fused_computation.7 | convolution fusion | flops 4841275392 | bytes 20447232 | tf_op jit(solution)/shard_map/sojcd,jdf->sojcf/dot_general | solution.py:144
  230.6 5.2 %convert_bitcast_fusion = bf16[8,4,2,32,1536]{4,3,1,0,2:T(8,128)(2,1)S(1)} fusion(bf16[8,4,2,32,768]{4,3,1,0,2:T(8,128)(2,1)S(1)} %fusion.2, bf16[2,768,1536]{2,1,0:T(8,128)(2,1)S(1)} %bitcast.125), kind=kOutput, calls=%fused_computation.13 | convolution fusion | flops 4834983936 | bytes 14155776 | tf_op jit(solution)/shard_map/sojcf,jfd->sojcd/dot_general | solution.py:147
  235.9 3.4 copy.72
  239.3 117.1 %reduce-scatter.2.cloned.1.call-done = bf16[1,4,64,1536]{3,2,1,0:T(8,128)(2,1)} async-done(((bf16[8,4,64,1536]{3,2,1,0:T(8,128)(2,1)}), bf16[1,4,64,1536]{3,2,1,0:T(8,128)(2,1)}) %reduce-scatter.2.cloned.1.call-update) | async-done | bytes 786448 | tf_op jit(solution)/shard_map/reduce_scatter | solution.py:148
  356.5 15.1 %all_to_all.20 = bf16[4,64,1536]{2,1,0:T(8,128)(2,1)S(1)} all-to-all(bf16[4,64,1536]{2,1,0:T(8,128)(2,1)} %bitcast.116), channel_id=1, replica_groups=mesh['dp'=8,'expert'=4] {'expert'}, dimensions={0} | all-to-all | bytes 1572864 | tf_op jit(solution)/shard_map/all_to_all | solution.py:157
  (89 shorter events, 40.0 us)
Async XLA Ops:
  6.5 18.9 %all-to-all-start = ((bf16[1,8,1,16,1536]{4,3,2,0,1:T(8,128)(2,1)}), bf16[1,8,1,16,1536]{4,3,2,0,1:T(8,128)(2,1)S(1)}, u32[]{:S(2)}, u32[]{:S(2)}) async-start(bf16[1,8,1,16,1536]{4,3,2,0,1:T(8,128)(2,1)} %bitcast.118), calls=%async_computation | async-start | bytes 786432 | tf_op jit(solution)/shard_map/all_to_all | solution.py:106
  13.8 342.7 %reduce-scatter.2.cloned.1.call-start = ((), (), s32[]{:S(2)}) async-start(), calls=%async_computation.4 | async-start | bytes 7077888 | tf_op jit(solution)/shard_map/reduce_scatter | solution.py:148
  14.7 0.6 copy-start.8
  25.9 7.4 %copy-start.2 = (bf16[128,1536]{1,0:T(8,128)(2,1)}, bf16[128,1536]{1,0:T(8,128)(2,1)S(1)}, u32[]{:S(2)}) copy-start(bf16[128,1536]{1,0:T(8,128)(2,1)S(1)} %fusion.35) | copy-start | bytes 1179652
  40.6 4.2 %copy-start = (bf16[2,64,24,64]{3,2,1,0:T(8,128)(2,1)S(1)}, bf16[2,64,24,64]{3,2,1,0:T(8,128)(2,1)}, u32[]{:S(2)}) copy-start(bf16[2,64,24,64]{3,2,1,0:T(8,128)(2,1)} %reshape.174) | copy-start | bytes 1179652
  40.6 4.2 %copy-start.5 = (f32[2,24,64]{2,1,0:T(8,128)S(1)}, f32[2,24,64]{2,1,0:T(8,128)}, u32[]{:S(2)}) copy-start(f32[2,24,64]{2,1,0:T(8,128)} %copy.56) | copy-start | bytes 36868
  40.7 4.2 %copy-start.7 = (pred[64,64]{1,0:T(8,128)(4,1)S(1)}, pred[64,64]{1,0:T(8,128)(4,1)}, u32[]{:S(2)}) copy-start(pred[64,64]{1,0:T(8,128)(4,1)} %iota_compare_fusion.4) | copy-start | bytes 12292
  44.4 2.3 copy-start.3
  44.4 2.3 copy-start.6
  52.4 3.5 copy-start.9
  70.6 21.6 %collective-permute-start = (bf16[1,4,64,1536]{3,2,1,0:T(8,128)(2,1)S(1)}, bf16[1,4,64,1536]{3,2,1,0:T(8,128)(2,1)S(1)}, u32[]{:S(2)}, u32[]{:S(2)}) collective-permute-start(bf16[1,4,64,1536]{3,2,1,0:T(8,128)(2,1)S(1)} %bitcast.112), channel_id=1, source_target_pairs={{0,4},{4,8},{8,12},{12,16},{16,20},{20,24},{24,28},{28,0},{1,5},{5... | collective-permute-start | bytes 2359304 | tf_op jit(solution)/shard_map/ppermute | solution.py:32
  92.2 32.6 %collective-permute-start.1 = (bf16[1,4,64,1536]{3,2,1,0:T(8,128)(2,1)S(1)}, bf16[1,4,64,1536]{3,2,1,0:T(8,128)(2,1)S(1)}, u32[]{:S(2)}, u32[]{:S(2)}) collective-permute-start(bf16[1,4,64,1536]{3,2,1,0:T(8,128)(2,1)S(1)} %collective-permute-done), channel_id=1, source_target_pairs={{0,4},{4,8},{8,12},{12,16},{16,20},{20,24},{24,28},{28,0},{1,5},{5... | collective-permute-start | bytes 2359304 | tf_op jit(solution)/shard_map/ppermute | solution.py:32
  92.2 35.1 %collective-permute-start.4 = (bf16[1,4,64,1536]{3,2,0,1:T(8,128)(2,1)S(1)}, bf16[1,4,64,1536]{3,2,0,1:T(8,128)(2,1)S(1)}, u32[]{:S(2)}, u32[]{:S(2)}) collective-permute-start(bf16[1,4,64,1536]{3,2,0,1:T(8,128)(2,1)S(1)} %all_to_all.19), channel_id=1, source_target_pairs={{4,0},{8,4},{12,8},{16,12},{20,16},{24,20},{28,24},{0,28},{5,1},{9... | collective-permute-start | bytes 2359304 | tf_op jit(solution)/shard_map/ppermute | solution.py:35
  124.8 2.5 copy-start.4
  124.8 35.3 %collective-permute-start.2 = (bf16[1,4,64,1536]{3,2,1,0:T(8,128)(2,1)S(1)}, bf16[1,4,64,1536]{3,2,1,0:T(8,128)(2,1)}, u32[]{:S(2)}, u32[]{:S(2)}) collective-permute-start(bf16[1,4,64,1536]{3,2,1,0:T(8,128)(2,1)S(1)} %collective-permute-done.1), channel_id=1, source_target_pairs={{0,4},{4,8},{8,12},{12,16},{16,20},{20,24},{24,28},{28,0},{1,5},{5... | collective-permute-start | bytes 2359304 | tf_op jit(solution)/shard_map/ppermute | solution.py:32
  127.3 35.4 %collective-permute-start.5 = (bf16[1,4,64,1536]{3,2,0,1:T(8,128)(2,1)S(1)}, bf16[1,4,64,1536]{3,2,0,1:T(8,128)(2,1)}, u32[]{:S(2)}, u32[]{:S(2)}) collective-permute-start(bf16[1,4,64,1536]{3,2,0,1:T(8,128)(2,1)S(1)} %collective-permute-done.4), channel_id=1, source_target_pairs={{4,0},{8,4},{12,8},{16,12},{20,16},{24,20},{28,24},{0,28},{5,1},{9... | collective-permute-start | bytes 2359304 | tf_op jit(solution)/shard_map/ppermute | solution.py:35
  160.2 34.9 %collective-permute-start.3 = (bf16[1,4,64,1536]{3,2,1,0:T(8,128)(2,1)}, bf16[1,4,64,1536]{3,2,1,0:T(8,128)(2,1)}, u32[]{:S(2)}, u32[]{:S(2)}) collective-permute-start(bf16[1,4,64,1536]{3,2,1,0:T(8,128)(2,1)} %collective-permute-done.2), channel_id=1, source_target_pairs={{0,4},{4,8},{8,12},{12,16},{16,20},{20,24},{24,28},{28,0},{1,5},{5... | collective-permute-start | bytes 2359304 | tf_op jit(solution)/shard_map/ppermute | solution.py:32
  162.8 43.4 %collective-permute-start.6 = (bf16[1,4,64,1536]{3,2,0,1:T(8,128)(2,1)}, bf16[1,4,64,1536]{3,2,0,1:T(8,128)(2,1)S(1)}, u32[]{:S(2)}, u32[]{:S(2)}) collective-permute-start(bf16[1,4,64,1536]{3,2,0,1:T(8,128)(2,1)} %collective-permute-done.5), channel_id=1, source_target_pairs={{4,0},{8,4},{12,8},{16,12},{20,16},{24,20},{28,24},{0,28},{5,1},{9... | collective-permute-start | bytes 2359304 | tf_op jit(solution)/shard_map/ppermute | solution.py:35
  213.5 8.7 %copy-start.1 = (bf16[8,4,64,1536]{3,2,1,0:T(8,128)(2,1)S(1)}, bf16[8,4,64,1536]{3,2,1,0:T(8,128)(2,1)}, u32[]{:S(2)}) copy-start(bf16[8,4,64,1536]{3,2,1,0:T(8,128)(2,1)} %gather_fusion) | copy-start | bytes 18874372
  213.5 17.1 %slice-start = ((s8[4718592]{0:T(1024)(128)(4,1)}), s8[4194304]{0:T(1024)(128)(4,1)S(1)}, s32[]{:S(2)}) async-start(s8[4718592]{0:T(1024)(128)(4,1)} %bitcast.124), calls=%async_computation.5 | async-start | bytes 8388608
  222.2 8.4 %slice-start.1 = ((s8[4718592]{0:T(1024)(128)(4,1)}), s8[524288]{0:T(1024)(128)(4,1)S(1)}, s32[]{:S(2)}) async-start(s8[4718592]{0:T(1024)(128)(4,1)} %bitcast.124), calls=%async_computation.6 | async-start | bytes 1048576
  239.3 132.3 %copy-start.10 = (s32[128]{0:T(128)S(1)}, s32[128]{0:T(128)}, u32[]{:S(2)}) copy-start(s32[128]{0:T(128)} %multiply_add_fusion) | copy-start | bytes 1540
Sparse Core Ops, SparseCore 0:
  239.4 116.9 reduce-scatter.1
